TPU v7x, 32 devices: a whole 2x2x4 slice. The times are simulated.
32 devices in a mesh: row: 8 (over z, x), col: 4 (over y, core).
Axes of the slice: x: 2, y: 2, z: 4, core: 2. Of those that a mesh axis runs over, the one named last changes fastest.
Arguments:
- features: bfloat16 [14336, 2048], P('row', 'col'), may hold values from -6 to 6
- neighbours: int32 [14336, 32], P('row'), may hold values from -1 to 127, as said below
- node_valid: int32 [14336], P('row'), may hold values from 0 to 1, as said below
- weight_one: bfloat16 [2048, 2048], P(None, 'col'), may hold values from -0.125 to 0.125
- gamma_one: float32 [2048], P('col'), may hold values from 0.25 to 1.75
- beta_one: float32 [2048], P('col'), may hold values from -0.5 to 0.5
- weight_two: bfloat16 [2048, 2048], P(None, 'col'), may hold values from -0.125 to 0.125
- gamma_two: float32 [2048], P('col'), may hold values from 0.25 to 1.75
- beta_two: float32 [2048], P('col'), may hold values from -0.5 to 0.5
- cotangent: bfloat16 [14336, 2048], P('row', 'col'), may hold values from -6 to 6
Outputs:
- output: float32 [14336, 2048], P('row', 'col')
- grad_features: float32 [14336, 2048], P('row', 'col')
- grad_weight_one: float32 [2048, 2048], P(None, 'col')
- grad_gamma_one: float32 [2048], P('col')
- grad_beta_one: float32 [2048], P('col')
- grad_weight_two: float32 [2048, 2048], P(None, 'col')
- grad_gamma_two: float32 [2048], P('col')
- grad_beta_two: float32 [2048], P('col')
Inputs may be any that keep to these rules, and one draw needn't show every extreme that they name: `neighbours`: entries >= 0 name valid nodes of the same slot; every valid node has 1 to 32 such entries, first in its list, the rest are -1; a padding row has only -1; some slot is full. `node_valid`: in each slot the valid nodes come first and number at least 40.
All inputs are finite; a program needn't handle non-finite values.
Results may differ from a plain program's by a relative error of at most 0.012.
Values may be sent and summed in bfloat16 or wider, within the bound.
No kernel may reach another device: no remote copies, remote signals or barrier semaphores. Data moves between devices by JAX's collectives and lax.ppermute only.
A program may use at most 128 MiB of HBM per device.

v0:
```python
import jax
import jax.numpy as jnp
from jax import lax
from jax.sharding import PartitionSpec as P

SLOT = 128
NBR = 32
EPSILON = 1e-05


def build_tiles(neighbours):
    entries_all = neighbours.reshape(-1, SLOT, NBR)

    def build(entries):
        columns = jnp.arange(SLOT, dtype=jnp.int32)
        hits = jnp.sum((entries[:, :, None] == columns[None, None, :]).astype(jnp.float32), axis=1)
        degree = jnp.sum((entries >= 0).astype(jnp.float32), axis=1)
        joined = hits + jnp.eye(SLOT, dtype=jnp.float32)
        return joined / (degree[:, None] + 1.0)

    tiles = lax.map(build, entries_all)
    return (tiles, jnp.diagonal(tiles, axis1=1, axis2=2))


def spread(values, tiles, self_weight):
    shaped = values.reshape(tiles.shape[0], SLOT, values.shape[1])
    summed = jnp.einsum("sij,sjd->sid", tiles, shaped, precision=lax.Precision.HIGHEST)
    return (summed + self_weight[:, :, None] * shaped).reshape(values.shape)


def spread_back(grads, tiles, self_weight):
    shaped = grads.reshape(tiles.shape[0], SLOT, grads.shape[1])
    summed = jnp.einsum("sji,sjd->sid", tiles, shaped, precision=lax.Precision.HIGHEST)
    return (summed + self_weight[:, :, None] * shaped).reshape(grads.shape)


def moments(linear, valid):
    total_valid, summed = lax.psum((jnp.sum(valid), jnp.sum(valid * linear, axis=0)), "row")
    mean = summed / total_valid
    centred = linear - mean
    variance = lax.psum(jnp.sum(valid * centred * centred, axis=0), "row") / total_valid
    return (total_valid, mean, variance)


def forward_layer(values, weight, gamma, beta, tiles, self_weight, valid):
    mixed = spread(values, tiles, self_weight).astype(jnp.bfloat16)
    gathered = lax.all_gather(mixed, "col", axis=1, tiled=True)
    linear = jnp.dot(gathered, weight, preferred_element_type=jnp.float32)
    total_valid, mean, variance = moments(linear, valid)
    inv_std = lax.rsqrt(variance + EPSILON)
    normed = (linear - mean) * inv_std
    before = gamma * normed + beta
    result = valid * jax.nn.silu(before)
    return (result, (gathered, normed, inv_std, before, total_valid))


def backward_layer(grad_result, weight, gamma, kept, tiles, self_weight, valid):
    gathered, normed, inv_std, before, total_valid = kept
    sigmoid_value = jax.nn.sigmoid(before)
    slope = sigmoid_value * (1.0 + before * (1.0 - sigmoid_value))
    grad_before = grad_result * valid * slope
    grad_beta, grad_gamma = lax.psum(
        (jnp.sum(grad_before, axis=0), jnp.sum(grad_before * normed, axis=0)), "row"
    )
    grad_normed = gamma * grad_before
    grad_linear = inv_std * (
        grad_normed - valid * (gamma * grad_beta + normed * gamma * grad_gamma) / total_valid
    )
    grad_low = grad_linear.astype(jnp.bfloat16)
    weight_terms = lax.dot_general(
        gathered, grad_low, (((0,), (0,)), ((), ())), preferred_element_type=jnp.float32
    )
    grad_weight = lax.psum(weight_terms, "row")
    partial_terms = lax.dot_general(
        grad_low, weight, (((1,), (1,)), ((), ())), preferred_element_type=jnp.float32
    )
    grad_mixed = lax.psum_scatter(partial_terms, "col", scatter_dimension=1, tiled=True)
    grad_values = spread_back(grad_mixed, tiles, self_weight)
    return (grad_values, grad_weight, grad_gamma, grad_beta)


def local(
    features,
    neighbours,
    node_valid,
    weight_one,
    gamma_one,
    beta_one,
    weight_two,
    gamma_two,
    beta_two,
    cotangent,
):
    tiles, self_weight = build_tiles(neighbours)
    valid = node_valid.astype(jnp.float32)[:, None]
    hidden, kept_one = forward_layer(
        features.astype(jnp.float32), weight_one, gamma_one, beta_one, tiles, self_weight, valid
    )
    output, kept_two = forward_layer(
        hidden, weight_two, gamma_two, beta_two, tiles, self_weight, valid
    )
    grad_hidden, grad_weight_two, grad_gamma_two, grad_beta_two = backward_layer(
        cotangent.astype(jnp.float32), weight_two, gamma_two, kept_two, tiles, self_weight, valid
    )
    grad_features, grad_weight_one, grad_gamma_one, grad_beta_one = backward_layer(
        grad_hidden, weight_one, gamma_one, kept_one, tiles, self_weight, valid
    )
    return (
        output,
        grad_features,
        grad_weight_one,
        grad_gamma_one,
        grad_beta_one,
        grad_weight_two,
        grad_gamma_two,
        grad_beta_two,
    )


def solution(mesh):
    placed = (
        P("row", "col"),
        P("row", None),
        P("row"),
        P(None, "col"),
        P("col"),
        P("col"),
        P(None, "col"),
        P("col"),
        P("col"),
        P("row", "col"),
    )
    return jax.shard_map(
        local,
        mesh=mesh,
        in_specs=placed,
        out_specs=(
            P("row", "col"),
            P("row", "col"),
            P(None, "col"),
            P("col"),
            P("col"),
            P(None, "col"),
            P("col"),
            P("col"),
        ),
        check_vma=False,
    )
```

profile of v0, /device:TPU:0, one launch (start us, length us, event | category | flops | bytes accessed | tf_op | source)
XLA Modules:
  0.0 855.5 jit_solution(2408295498759646820)
XLA Ops:
  7.3 2.3 copy.23
  9.6 27.6 %while.10 = (s32[]{:T(128)}, f32[14,128,128]{2,1,0:T(8,128)S(1)}, s32[14,128,32]{2,1,0:T(8,128)}, s32[]{:T(128)}) while((s32[]{:T(128)}, f32[14,128,128]{2,1,0:T(8,128)S(1)}, s32[14,128,32]{2,1,0:T(8,128)}, s32[]{:T(128)}) %tuple.47), condition=%wide.region_3.4_spmd, body=%wide.region_0.3_spmd.sunk | while | flops 1634306 | bytes 247877 | solution.py:21
  37.2 4.7 copy.24
  43.7 5.1 add_convert_fusion.1
  49.5 54.5 %all-gather.3.cloned.1.call-done = bf16[1792,2048]{1,0:T(8,128)(2,1)} async-done(((bf16[1792,512]{1,0:T(8,128)(2,1)}), bf16[1792,2048]{1,0:T(8,128)(2,1)}) %all-gather.3.cloned.1.call-update) | async-done | bytes 7340048 | tf_op jit(solution)/shard_map/all_gather | solution.py:47
  104.0 9.5 %multiply_reduce_fusion.3 = (f32[512]{0:T(512)S(1)}, f32[1792,512]{1,0:T(8,128)}) fusion(f32[1792]{0:T(1024)S(1)} %convert_element_type.41, bf16[1792,2048]{1,0:T(8,128)(2,1)} %all-gather.3.cloned.1.call-done, bf16[2048,512]{1,0:T(8,128)(2,1)} %param.15), kind=kOutput, calls=%fused_computation.29 | convolution fusion | flops 3759930880 | bytes 13116416 | tf_op jit(solution)/shard_map/dot_general | solution.py:48
  113.5 22.0 %all-reduce.2 = (f32[512]{0:T(512)S(1)}, f32[]{:T(128)}) all-reduce(f32[512]{0:T(512)S(1)} %get-tuple-element.49, f32[]{:T(128)} %convert_reduce_fusion.2), channel_id=1, replica_groups=mesh['row'=8,'col'=4] {'row'}, use_global_device_ids=true, to_apply=%region_5.6 | all-reduce | flops 513 | bytes 4104 | tf_op jit(solution)/shard_map/psum | solution.py:38
  136.0 2.6 fusion.2
  138.6 17.1 %psum.82 = f32[512]{0:T(512)S(1)} all-reduce(f32[512]{0:T(512)S(1)} %fusion.2), channel_id=1, replica_groups=mesh['row'=8,'col'=4] {'row'}, use_global_device_ids=true, to_apply=%region_9.10 | all-reduce | flops 512 | bytes 4096 | tf_op jit(solution)/shard_map/psum | solution.py:41
  156.3 3.0 multiply_multiply_fusion.4
  159.4 4.5 add_convert_fusion
  164.1 50.0 %all-gather.5.cloned.1.call-done = bf16[1792,2048]{1,0:T(8,128)(2,1)} async-done(((bf16[1792,512]{1,0:T(8,128)(2,1)}), bf16[1792,2048]{1,0:T(8,128)(2,1)}) %all-gather.5.cloned.1.call-update) | async-done | bytes 7340048 | tf_op jit(solution)/shard_map/all_gather | solution.py:47
  214.1 8.9 %multiply_reduce_fusion.2 = (f32[512]{0:T(512)S(1)}, f32[1792,512]{1,0:T(8,128)}) fusion(f32[1792]{0:T(1024)S(1)} %convert_element_type.41, bf16[1792,2048]{1,0:T(8,128)(2,1)} %all-gather.5.cloned.1.call-done, bf16[2048,512]{1,0:T(8,128)(2,1)S(1)} %copy-done), kind=kOutput, calls=%fused_computation.25 | convolution fusion | flops 3759930880 | bytes 13116416 | tf_op jit(solution)/shard_map/dot_general | solution.py:48
  223.0 21.5 %psum.83 = f32[512]{0:T(512)S(1)} all-reduce(f32[512]{0:T(512)S(1)} %get-tuple-element.51), channel_id=1, replica_groups=mesh['row'=8,'col'=4] {'row'}, use_global_device_ids=true, to_apply=%region_11.12 | all-reduce | flops 512 | bytes 4096 | tf_op jit(solution)/shard_map/psum | solution.py:38
  245.1 2.6 fusion.3
  247.7 17.1 %psum.84 = f32[512]{0:T(512)S(1)} all-reduce(f32[512]{0:T(512)S(1)} %fusion.3), channel_id=1, replica_groups=mesh['row'=8,'col'=4] {'row'}, use_global_device_ids=true, to_apply=%region_13.14 | all-reduce | flops 512 | bytes 4096 | tf_op jit(solution)/shard_map/psum | solution.py:41
  265.4 6.3 fusion.6
  271.7 19.1 %all-reduce.1 = (f32[512]{0:T(512)S(1)}, f32[512]{0:T(512)S(1)}) all-reduce(f32[512]{0:T(512)S(1)} %get-tuple-element.29, f32[512]{0:T(512)S(1)} %get-tuple-element.28), channel_id=1, replica_groups=mesh['row'=8,'col'=4] {'row'}, use_global_device_ids=true, to_apply=%region_17.18 | all-reduce | flops 1024 | bytes 8192 | tf_op jit(solution)/shard_map/psum | solution.py:62
  290.8 4.5 multiply_convert_fusion.1
  296.6 7.2 fusion.8
  304.1 109.0 %reduce-scatter.3.cloned.1.call-done = f32[1792,512]{1,0:T(8,128)} async-done(((f32[1792,2048]{1,0:T(8,128)}), f32[1792,512]{1,0:T(8,128)}) %reduce-scatter.3.cloned.1.call-update) | async-done | bytes 3670032 | tf_op jit(solution)/shard_map/reduce_scatter | solution.py:77
  413.1 6.8 multiply_add_fusion.1
  419.9 3.7 fusion.5
  423.7 21.3 %all-reduce = (f32[512]{0:T(512)S(1)}, f32[512]{0:T(512)S(1)}) all-reduce(f32[512]{0:T(512)S(1)} %get-tuple-element.27, f32[512]{0:T(512)S(1)} %get-tuple-element.26), channel_id=1, replica_groups=mesh['row'=8,'col'=4] {'row'}, use_global_device_ids=true, to_apply=%region_22.23 | all-reduce | flops 1024 | bytes 8192 | tf_op jit(solution)/shard_map/psum | solution.py:62
  445.0 4.7 multiply_convert_fusion
  449.8 7.3 fusion.9
  458.5 9.9 %fusion.11 = f32[2048,512]{1,0:T(8,128)} fusion(bf16[1792,2048]{1,0:T(8,128)(2,1)} %all-gather.5.cloned.1.call-done, bf16[1792,512]{1,0:T(8,128)(2,1)S(1)} %copy-done.5), kind=kOutput, calls=%fused_computation.44 | convolution fusion | flops 3758096384 | bytes 13369344 | tf_op jit(solution)/shard_map/dot_general | solution.py:70
  468.4 10.5 %fusion.10 = f32[2048,512]{1,0:T(8,128)} fusion(bf16[1792,2048]{1,0:T(8,128)(2,1)} %all-gather.3.cloned.1.call-done, bf16[1792,512]{1,0:T(8,128)(2,1)S(1)} %copy-done.7), kind=kOutput, calls=%fused_computation.43 | convolution fusion | flops 3758096384 | bytes 13369344 | tf_op jit(solution)/shard_map/dot_general | solution.py:70
  479.0 87.5 %reduce-scatter.5.cloned.1.call-done = f32[1792,512]{1,0:T(8,128)} async-done(((f32[1792,2048]{1,0:T(8,128)}), f32[1792,512]{1,0:T(8,128)}) %reduce-scatter.5.cloned.1.call-update) | async-done | bytes 3670032 | tf_op jit(solution)/shard_map/reduce_scatter | solution.py:77
  566.5 8.5 multiply_add_fusion
  575.0 267.1 %all-reduce.6.cloned.1.call-done = (f32[2048,512]{1,0:T(8,128)}, f32[2048,512]{1,0:T(8,128)}) async-done(((f32[2048,512]{1,0:T(8,128)}, f32[2048,512]{1,0:T(8,128)}), (f32[2048,512]{1,0:T(8,128)}, f32[2048,512]{1,0:T(8,128)})) %all-reduce.6.cloned.1.call-update) | async-done | bytes 8388624 | tf_op jit(solution)/shard_map/psum | solution.py:73
  842.1 4.8 copy.41
  (115 shorter events, 37.2 us)
Async XLA Ops:
  7.2 207.0 %copy-start = (bf16[2048,512]{1,0:T(8,128)(2,1)S(1)}, bf16[2048,512]{1,0:T(8,128)(2,1)}, u32[]{:S(2)}) copy-start(bf16[2048,512]{1,0:T(8,128)(2,1)} %param.18) | copy-start | bytes 6291460
  7.2 96.8 %all-gather.3.cloned.1.call-start = ((), (), s32[]{:S(2)}) async-start(), calls=%async_computation.2 | async-start | bytes 9175040 | tf_op jit(solution)/shard_map/all_gather | solution.py:47
  41.8 7.0 copy-start.8
  48.8 165.3 %all-gather.5.cloned.1.call-start = ((), (), s32[]{:S(2)}) async-start(), calls=%async_computation.3 | async-start | bytes 9175040 | tf_op jit(solution)/shard_map/all_gather | solution.py:47
  113.5 42.8 %copy-start.9 = (f32[512]{0:T(512)S(1)}, f32[512]{0:T(512)}, u32[]{:S(2)}) copy-start(f32[512]{0:T(512)} %param.16) | copy-start | bytes 6148
  113.5 42.8 %copy-start.11 = (f32[512]{0:T(512)S(1)}, f32[512]{0:T(512)}, u32[]{:S(2)}) copy-start(f32[512]{0:T(512)} %param.17) | copy-start | bytes 6148
  163.9 249.3 %reduce-scatter.3.cloned.1.call-start = ((), (), s32[]{:S(2)}) async-start(), calls=%async_computation.4 | async-start | bytes 18350080 | tf_op jit(solution)/shard_map/reduce_scatter | solution.py:77
  223.0 42.3 %copy-start.10 = (f32[512]{0:T(512)S(1)}, f32[512]{0:T(512)}, u32[]{:S(2)}) copy-start(f32[512]{0:T(512)} %param.19) | copy-start | bytes 6148
  223.0 42.3 %copy-start.12 = (f32[512]{0:T(512)S(1)}, f32[512]{0:T(512)}, u32[]{:S(2)}) copy-start(f32[512]{0:T(512)} %param.20) | copy-start | bytes 6148
  290.8 4.5 copy-start.13
  290.8 4.6 copy-start.15
  295.3 1.2 copy-start.4
  303.8 262.6 %reduce-scatter.5.cloned.1.call-start = ((), (), s32[]{:S(2)}) async-start(), calls=%async_computation.5 | async-start | bytes 18350080 | tf_op jit(solution)/shard_map/reduce_scatter | solution.py:77
  413.1 6.8 copy-start.2
  445.0 4.7 copy-start.14
  445.0 4.7 copy-start.16
  445.0 4.7 copy-start.17
  449.7 7.3 copy-start.6
  457.0 1.5 copy-start.5
  457.0 385.1 %all-reduce.6.cloned.1.call-start = ((), (), s32[]{:S(2)}) async-start(), calls=%async_computation.6 | async-start | bytes 16777216 | tf_op jit(solution)/shard_map/psum | solution.py:73
  458.5 9.9 %copy-start.7 = (bf16[1792,512]{1,0:T(8,128)(2,1)S(1)}, bf16[1792,512]{1,0:T(8,128)(2,1)}, u32[]{:S(2)}) copy-start(bf16[1792,512]{1,0:T(8,128)(2,1)} %copy-done.6) | copy-start | bytes 5505028
  842.1 4.8 copy-start.3
  842.1 6.8 copy-start.1
Sparse Core Ops, SparseCore 0:
  48.9 55.0 all-gather.2
  164.0 50.1 all-gather.4
  303.9 109.1 reduce-scatter.2
  457.2 109.2 reduce-scatter.4
  571.0 271.0 all-reduce.5
where the time goes:
time: 857 us; the launch traced here: 855 us
  waiting for transfers between devices  568 us (66%)
  blocking collectives  118 us (14%)
  matrix products  78.2 us (9%)
  other arithmetic  57.2 us (7%)
  local copies, waits for them, and re-layouts  18.1 us (2%)
  between operations  14 us (2%)
    psum x1, waiting for transfers between devices, backward_layer(): grad_weight = lax.psum(weight_terms, 'row')  267 us
    reduce_scatter x2, waiting for transfers between devices, backward_layer(): lax.psum_scatter(partial_terms, 'col', scatter_dimension=1, tiled=True)  197 us
    all_gather x2, waiting for transfers between devices, forward_layer(): gathered = lax.all_gather(mixed, 'col', axis=1, tiled=True)  105 us
    psum x2, blocking collectives, moments(): lax.psum((jnp.sum(valid), jnp.sum(valid * linear, axis=0)), 'row')  43.4 us
    psum x2, blocking collectives, backward_layer(): lax.psum((jnp.sum(grad_before, axis=0), jnp.sum(grad_before * normed, axi...  40.5 us
    psum x2, blocking collectives, moments(): lax.psum(jnp.sum(valid * centred * centred, axis=0), 'row') / total_valid  34.3 us
    dot_general x2, matrix products, backward_layer(): lax.dot_general(gathered, grad_low, (((0,), (0,)), ((), ())), preferred_e...  20.4 us
    dot_general x2, matrix products, forward_layer(): linear = jnp.dot(gathered, weight, preferred_element_type=jnp.float32)  18.4 us
  transfers between devices with their start and end apart: 5, of which 5 were waited for; matrix products, arithmetic and copies ran while one was open for 3% of the time, Pallas kernels for 0%

commit v1 on v0

--- a/solution.py
+++ b/solution.py
@@ -70,7 +70,7 @@
     weight_terms = lax.dot_general(
         gathered, grad_low, (((0,), (0,)), ((), ())), preferred_element_type=jnp.float32
     )
-    grad_weight = lax.psum(weight_terms, "row")
+    grad_weight = jnp.sum(lax.all_gather(weight_terms, "row"), axis=0)
     partial_terms = lax.dot_general(
         grad_low, weight, (((1,), (1,)), ((), ())), preferred_element_type=jnp.float32
     )

time: 857 us -> 1840 us (2.15)
  waiting for transfers between devices: 568 us -> 1480 us
  blocking collectives: 118 us -> 154 us
  other arithmetic: 57.2 us -> 91.1 us
    all_gather x0 -> x2, waiting for transfers between devices: none -> 1180 us  [backward_layer(): grad_weight = jnp.sum(lax.all_gather(weight_terms, 'row'), axis=0)]
    psum x1 -> x0, waiting for transfers between devices: 267 us -> none  [backward_layer(): grad_weight = lax.psum(weight_terms, 'row')]
    psum x2, blocking collectives: 40.5 us -> 76.5 us  [backward_layer(): lax.psum((jnp.sum(grad_before, axis=0), jnp.sum(grad_before * normed, axi...]
    reduce_sum x0 -> x2, other arithmetic: none -> 33.1 us  [backward_layer(): grad_weight = jnp.sum(lax.all_gather(weight_terms, 'row'), axis=0)]
  transfers between devices with their start and end apart: 5 -> 6, of which waited for: 5 -> 6; matrix products, arithmetic and copies ran while one was open for 3% -> 4% of each run, Pallas kernels for 0% -> 0%
where the time goes in v1:
time: 1840 us; the launch traced here: 1830 us
  waiting for transfers between devices  1480 us (80%)
  blocking collectives  154 us (8%)
  other arithmetic  91.1 us (5%)
  matrix products  76.3 us (4%)
    all_gather x2, waiting for transfers between devices, backward_layer(): grad_weight = jnp.sum(lax.all_gather(weight_terms, 'row'), axis=0)  1180 us
    reduce_scatter x2, waiting for transfers between devices, backward_layer(): lax.psum_scatter(partial_terms, 'col', scatter_dimension=1, tiled=True)  195 us
    all_gather x2, waiting for transfers between devices, forward_layer(): gathered = lax.all_gather(mixed, 'col', axis=1, tiled=True)  104 us
    psum x2, blocking collectives, backward_layer(): lax.psum((jnp.sum(grad_before, axis=0), jnp.sum(grad_before * normed, axi...  76.5 us
    psum x2, blocking collectives, moments(): lax.psum((jnp.sum(valid), jnp.sum(valid * linear, axis=0)), 'row')  43.5 us
  transfers between devices with their start and end apart: 6, of which 6 were waited for; matrix products, arithmetic and copies ran while one was open for 4% of the time, Pallas kernels for 0%

profile of v1, /device:TPU:0, one launch (start us, length us, event | category | flops | bytes accessed | tf_op | source)
XLA Modules:
  0.0 1831.4 jit_solution(17772845330971338407)
XLA Ops:
  9.6 27.6 %while.10 = (s32[]{:T(128)}, f32[14,128,128]{2,1,0:T(8,128)S(1)}, s32[14,128,32]{2,1,0:T(8,128)}, s32[]{:T(128)}) while((s32[]{:T(128)}, f32[14,128,128]{2,1,0:T(8,128)S(1)}, s32[14,128,32]{2,1,0:T(8,128)}, s32[]{:T(128)}) %tuple.47), condition=%wide.region_3.4_spmd, body=%wide.region_0.3_spmd.sunk | while | flops 1634306 | bytes 247869 | solution.py:21
  37.2 4.7 copy.24
  43.7 5.1 add_convert_fusion.1
  49.4 54.5 %all-gather.7.cloned.1.call-done = bf16[1792,2048]{1,0:T(8,128)(2,1)} async-done(((bf16[1792,512]{1,0:T(8,128)(2,1)}), bf16[1792,2048]{1,0:T(8,128)(2,1)}) %all-gather.7.cloned.1.call-update) | async-done | bytes 7340048 | tf_op jit(solution)/shard_map/all_gather | solution.py:47
  103.9 9.5 multiply_reduce_fusion.3
  113.5 22.0 %all-reduce.2 = (f32[512]{0:T(512)S(1)}, f32[]{:T(128)}) all-reduce(f32[512]{0:T(512)S(1)} %get-tuple-element.47, f32[]{:T(128)} %convert_reduce_fusion.2), channel_id=1, replica_groups=mesh['row'=8,'col'=4] {'row'}, use_global_device_ids=true, to_apply=%region_5.6 | all-reduce | flops 513 | bytes 4104 | tf_op jit(solution)/shard_map/psum | solution.py:38
  138.7 17.1 psum.68
  156.6 3.0 multiply_multiply_fusion.4
  159.6 4.5 add_convert_fusion
  164.6 49.8 %all-gather.9.cloned.1.call-done = bf16[1792,2048]{1,0:T(8,128)(2,1)} async-done(((bf16[1792,512]{1,0:T(8,128)(2,1)}), bf16[1792,2048]{1,0:T(8,128)(2,1)}) %all-gather.9.cloned.1.call-update) | async-done | bytes 7340048 | tf_op jit(solution)/shard_map/all_gather | solution.py:47
  214.4 8.9 multiply_reduce_fusion.2
  223.3 21.5 %psum.69 = f32[512]{0:T(512)S(1)} all-reduce(f32[512]{0:T(512)S(1)} %get-tuple-element.49), channel_id=1, replica_groups=mesh['row'=8,'col'=4] {'row'}, use_global_device_ids=true, to_apply=%region_11.12 | all-reduce | flops 512 | bytes 4096 | tf_op jit(solution)/shard_map/psum | solution.py:38
  245.4 2.6 fusion.3
  248.0 17.1 psum.70
  265.8 6.3 fusion.6
  272.1 19.1 %all-reduce.1 = (f32[512]{0:T(512)S(1)}, f32[512]{0:T(512)S(1)}) all-reduce(f32[512]{0:T(512)S(1)} %get-tuple-element.29, f32[512]{0:T(512)S(1)} %get-tuple-element.28), channel_id=1, replica_groups=mesh['row'=8,'col'=4] {'row'}, use_global_device_ids=true, to_apply=%region_17.18 | all-reduce | flops 1024 | bytes 8192 | tf_op jit(solution)/shard_map/psum | solution.py:62
  291.2 4.6 multiply_convert_fusion.1
  297.1 7.2 fusion.8
  305.9 9.8 fusion.11
  315.9 97.8 %reduce-scatter.3.cloned.1.call-done = f32[1792,512]{1,0:T(8,128)} async-done(((f32[1792,2048]{1,0:T(8,128)}), f32[1792,512]{1,0:T(8,128)}) %reduce-scatter.3.cloned.1.call-update) | async-done | bytes 3670032 | tf_op jit(solution)/shard_map/reduce_scatter | solution.py:77
  413.7 6.8 multiply_add_fusion.1
  420.5 3.7 fusion.5
  424.3 57.4 %all-reduce = (f32[512]{0:T(512)S(1)}, f32[512]{0:T(512)S(1)}) all-reduce(f32[512]{0:T(512)S(1)} %get-tuple-element.27, f32[512]{0:T(512)S(1)} %get-tuple-element.26), channel_id=1, replica_groups=mesh['row'=8,'col'=4] {'row'}, use_global_device_ids=true, to_apply=%region_22.23 | all-reduce | flops 1024 | bytes 8192 | tf_op jit(solution)/shard_map/psum | solution.py:62
  481.7 4.9 multiply_convert_fusion
  486.6 7.2 fusion.9
  494.2 8.8 fusion.10
  503.0 551.1 %all-gather.13.cloned.1.call-done = f32[16384,512]{1,0:T(8,128)} async-done(((f32[2048,512]{1,0:T(8,128)}), f32[16384,512]{1,0:T(8,128)}) %all-gather.13.cloned.1.call-update) | async-done | bytes 33554448 | tf_op jit(solution)/shard_map/all_gather | solution.py:73
  1054.0 17.9 reduce_sum.133
  1071.9 97.5 %reduce-scatter.5.cloned.1.call-done = f32[1792,512]{1,0:T(8,128)} async-done(((f32[1792,2048]{1,0:T(8,128)}), f32[1792,512]{1,0:T(8,128)}) %reduce-scatter.5.cloned.1.call-update) | async-done | bytes 3670032 | tf_op jit(solution)/shard_map/reduce_scatter | solution.py:77
  1169.4 8.5 multiply_add_fusion
  1177.9 631.2 %all-gather.11.cloned.1.call-done = f32[16384,512]{1,0:T(8,128)} async-done(((f32[2048,512]{1,0:T(8,128)}), f32[16384,512]{1,0:T(8,128)}) %all-gather.11.cloned.1.call-update) | async-done | bytes 33554448 | tf_op jit(solution)/shard_map/all_gather | solution.py:73
  1809.1 15.2 reduce_sum.132
  (112 shorter events, 41.0 us)
Async XLA Ops:
  7.2 207.2 %copy-start = (bf16[2048,512]{1,0:T(8,128)(2,1)S(1)}, bf16[2048,512]{1,0:T(8,128)(2,1)}, u32[]{:S(2)}) copy-start(bf16[2048,512]{1,0:T(8,128)(2,1)} %param.18) | copy-start | bytes 6291460
  7.2 96.8 %all-gather.7.cloned.1.call-start = ((), (), s32[]{:S(2)}) async-start(), calls=%async_computation.2 | async-start | bytes 9175040 | tf_op jit(solution)/shard_map/all_gather | solution.py:47
  41.8 7.0 copy-start.5
  48.8 165.6 %all-gather.9.cloned.1.call-start = ((), (), s32[]{:S(2)}) async-start(), calls=%async_computation.3 | async-start | bytes 9175040 | tf_op jit(solution)/shard_map/all_gather | solution.py:47
  113.5 43.1 %copy-start.6 = (f32[512]{0:T(512)S(1)}, f32[512]{0:T(512)}, u32[]{:S(2)}) copy-start(f32[512]{0:T(512)} %param.16) | copy-start | bytes 6148
  113.5 43.1 %copy-start.8 = (f32[512]{0:T(512)S(1)}, f32[512]{0:T(512)}, u32[]{:S(2)}) copy-start(f32[512]{0:T(512)} %param.17) | copy-start | bytes 6148
  164.1 249.6 %reduce-scatter.3.cloned.1.call-start = ((), (), s32[]{:S(2)}) async-start(), calls=%async_computation.4 | async-start | bytes 18350080 | tf_op jit(solution)/shard_map/reduce_scatter | solution.py:77
  223.3 42.5 %copy-start.7 = (f32[512]{0:T(512)S(1)}, f32[512]{0:T(512)}, u32[]{:S(2)}) copy-start(f32[512]{0:T(512)} %param.19) | copy-start | bytes 6148
  223.3 42.6 %copy-start.9 = (f32[512]{0:T(512)S(1)}, f32[512]{0:T(512)}, u32[]{:S(2)}) copy-start(f32[512]{0:T(512)} %param.20) | copy-start | bytes 6148
  291.2 4.7 copy-start.10
  291.2 4.7 copy-start.12
  295.9 1.2 copy-start.3
  304.4 1.5 copy-start.4
  304.4 749.6 %all-gather.13.cloned.1.call-start = ((), (), s32[]{:S(2)}) async-start(), calls=%async_computation.7 | async-start | bytes 37748736 | tf_op jit(solution)/shard_map/all_gather | solution.py:73
  315.6 853.8 %reduce-scatter.5.cloned.1.call-start = ((), (), s32[]{:S(2)}) async-start(), calls=%async_computation.5 | async-start | bytes 18350080 | tf_op jit(solution)/shard_map/reduce_scatter | solution.py:77
  413.7 6.8 copy-start.2
  481.7 4.9 copy-start.11
  481.7 5.0 copy-start.13
  481.7 4.9 copy-start.14
  493.9 1315.3 %all-gather.11.cloned.1.call-start = ((), (), s32[]{:S(2)}) async-start(), calls=%async_computation.6 | async-start | bytes 37748736 | tf_op jit(solution)/shard_map/all_gather | solution.py:73
  1809.1 15.2 copy-start.1
Sparse Core Ops, SparseCore 0:
  48.9 55.0 all-gather.6
  164.2 50.1 all-gather.8
  304.5 109.1 reduce-scatter.2
  415.7 638.3 all-gather.12
  1056.5 112.9 reduce-scatter.4
  1171.4 637.7 all-gather.10
